TPU v7x, 32 devices: a whole 2x2x4 slice. The times are simulated.
32 devices in a mesh: feeder: 8 (over z, core), tm: 4 (over y, x).
Axes of the slice: x: 2, y: 2, z: 4, core: 2. Of those that a mesh axis runs over, the one named last changes fastest.
Arguments:
- node_load: bfloat16 [128, 64, 24, 512], P('feeder', None, 'tm'), may hold values from -6 to 6
- drive_map: bfloat16 [128, 512, 256], P('feeder'), may hold values from -0.25 to 0.25
- decay_rate: float32 [128, 24, 256], P('feeder', 'tm'), may hold values from 0.45 to 1
- counts: int32 [128], P('feeder'), may hold values from 64 to 256
- out_map: float32 [128, 2, 256], P('feeder'), may hold values from -0.375 to 0.375
- area_of: int32 [128, 1], replicated, may hold values from 0 to 7; in each aligned block of 16 rows (0 to 15, 16 to 31, ...) at most 2 rows name the same one
- head_bus: int32 [128], replicated, may hold values from 0 to 255
- rule_of: int32 [128], replicated, may hold values from 0 to 15
- rule_knots: int32 [16, 8], replicated, may hold values from -3200 to 2400, as said below
- levels: int32 [16, 8], replicated, may hold values from -1000 to 1000
- sensitivity: float32 [8, 2, 256, 256], P('feeder'), may hold values from -0.6 to 0.6
Outputs:
- setpoints: float32 [128, 24, 64], P('feeder', 'tm')
Inputs may be any that keep to these rules, and one draw needn't show every extreme that they name: `area_of`: in each aligned block of 16 feeders no area is named by more than 2 feeders, a bound that some block reaches. `rule_knots`: each row strictly increasing, neighbouring breakpoints 200 to 800 apart.
All inputs are finite; a program needn't handle non-finite values.
Results may differ from a plain program's by a relative error of at most 0.00045.
Values sent between devices are 32-bit elements; how exact they have to be, the bound alone decides.
A program may use at most 64 MiB of HBM per device.

v0:
```python
import functools

import jax
import jax.numpy as jnp
from jax import lax
from jax.experimental import pallas as pl
from jax.experimental.pallas import tpu as pltpu
from jax.sharding import PartitionSpec as P

HIGH = lax.Precision.HIGHEST
NT = (((1,), (1,)), ((), ()))
MESH = pl.DeviceIdType.MESH
UNROLL = 8


def split(value):
    upper = value.astype(jnp.bfloat16).astype(jnp.float32)
    return upper, value - upper


def kernel(
    groups,
    turns,
    load_hbm,
    map_hbm,
    decay_ref,
    counts_ref,
    out_map_ref,
    area_ref,
    bus_ref,
    rule_ref,
    knots_ref,
    levels_ref,
    sens_hbm,
    out_ref,
    load_ref,
    map_ref,
    sens_ref,
    later_decay,
    pair_send,
    pair_recv,
    weight_ref,
    state_ref,
    column_ref,
    rule_vals,
    flow_ref,
    flow_send,
    flow_recv,
    volt_send,
    volt_recv,
    load_sem,
    map_sem,
    sens_sem,
    decay_sems,
    pair_sems,
    flow_sems,
    volt_sems,
):
    group, turn = lax.axis_index("feeder"), lax.axis_index("tm")
    per_dev, span, scen, nodes = load_ref.shape
    width = map_ref.shape[2]
    half = per_dev // 2
    couples = span // 2
    feeders = bus_ref.shape[1]
    buses = sens_ref.shape[1]
    rows = weight_ref.shape[1] // per_dev
    later_rows = rows // 2
    piece = couples * 2 * half

    sens_copy = pltpu.make_async_copy(sens_hbm.at[0], sens_ref, sens_sem)
    sens_copy.start()

    def load_copies(f):
        return (
            pltpu.make_async_copy(load_hbm.at[f], load_ref.at[f], load_sem.at[f]),
            pltpu.make_async_copy(map_hbm.at[f], map_ref.at[f], map_sem.at[f]),
        )

    def start_loads(f, carry):
        for copy in load_copies(f):
            copy.start()
        return carry

    lax.fori_loop(0, per_dev, start_loads, 0)

    barrier = pltpu.get_barrier_semaphore()
    for step in range(1, turns):
        pl.semaphore_signal(
            barrier,
            inc=1,
            device_id=(group, lax.rem(turn + step, turns)),
            device_id_type=MESH,
        )
    for step in range(1, groups):
        pl.semaphore_signal(
            barrier,
            inc=1,
            device_id=(lax.rem(group + step, groups), turn),
            device_id_type=MESH,
        )

    def decay_copy(step):
        return pltpu.make_async_remote_copy(
            src_ref=decay_ref,
            dst_ref=later_decay.at[step - 1],
            send_sem=decay_sems.at[0, step - 1],
            recv_sem=decay_sems.at[1, step - 1],
            device_id=(group, turn - step),
            device_id_type=MESH,
        )

    bus_ids = lax.broadcasted_iota(jnp.int32, (buses, feeders), 0)
    owned = (bus_ids == bus_ref[...]) & (area_ref[...] == group)
    hot = jnp.where(owned, 1.0, 0.0)
    hot_rows = hot.T.astype(jnp.bfloat16)
    hot = hot.astype(jnp.bfloat16)
    sens_copy.wait()
    for k in range(2):
        picked = sum(
            lax.dot_general(
                hot_rows, term.astype(jnp.bfloat16), NT, preferred_element_type=jnp.float32
            )
            for term in split(sens_ref[k])
        )
        pairs = sum(
            jnp.dot(term.astype(jnp.bfloat16), hot, preferred_element_type=jnp.float32)
            for term in split(picked)
        )
        pair_send[:, k] = pairs.reshape(groups, per_dev, feeders)

    pl.semaphore_wait(barrier, turns + groups - 2)

    for step in range(1, turns):

        @pl.when(turn >= step)
        def _():
            decay_copy(step).start()

    def pair_copy(step):
        target = lax.rem(group + step, groups)
        return pltpu.make_async_remote_copy(
            src_ref=pair_send.at[target],
            dst_ref=pair_recv.at[step - 1],
            send_sem=pair_sems.at[0, step - 1],
            recv_sem=pair_sems.at[1, step - 1],
            device_id=(target, turn),
            device_id_type=MESH,
        )

    for step in range(1, groups):
        pair_copy(step).start()

    rules = knots_ref.shape[1]
    rule_ids = lax.broadcasted_iota(jnp.int32, (rules, feeders), 0)
    rule_hot = jnp.where(rule_ids == rule_ref[...], 1.0, 0.0)
    table = jnp.concatenate(
        [knots_ref[...].astype(jnp.float32), levels_ref[...].astype(jnp.float32)], axis=0
    )
    chosen = jnp.dot(table, rule_hot, precision=HIGH, preferred_element_type=jnp.float32)
    rule_vals[...] = (chosen / 1000.0).T

    member = lax.broadcasted_iota(jnp.int32, (per_dev, width), 0)
    state_ids = lax.broadcasted_iota(jnp.int32, (per_dev, width), 1)
    limit = jnp.zeros((per_dev, width), jnp.int32)
    for f in range(per_dev):
        limit = jnp.where(member == f, counts_ref[f], limit)
    maps = [jnp.where(state_ids < limit, out_map_ref[:, k, :], 0.0) for k in range(2)]

    def put_rows(row, value):
        for lane in range(width // 128):
            weight_ref[lane, pl.ds(row, per_dev, stride=rows), :] = value[
                :, lane * 128 : (lane + 1) * 128
            ]

    parts = [split(m) for m in maps]
    columns = [p[0] for p in parts] + [p[1] for p in parts]
    blank = jnp.zeros((128 - 4 * per_dev, width), jnp.float32)
    columns = jnp.concatenate(columns + [blank], axis=0).T.astype(jnp.bfloat16)
    lane_ids = lax.rem(lax.broadcasted_iota(jnp.int32, (1, 128), 1), per_dev)
    for f in range(per_dev):
        own = columns * jnp.where(lane_ids == f, 1.0, 0.0).astype(jnp.bfloat16)
        for copy in range(2):
            first = (2 * f + copy) * width
            column_ref[first : first + width] = own
    def feeder_states(f, carry):
        for copy in load_copies(f):
            copy.wait()
        drive = jnp.dot(
            load_ref[f].reshape(span * scen, nodes),
            map_ref[f],
            preferred_element_type=jnp.float32,
        )
        states = [drive[:scen]]
        for t in range(1, span):
            retain = decay_ref[t, pl.ds(f, 1), :]
            states.append(retain * states[-1] + drive[t * scen : (t + 1) * scen])
        upper, lower = split(jnp.concatenate(states, axis=0))
        first = pl.multiple_of(2 * f * width, 128)
        state_ref[:, pl.ds(first, width)] = upper.astype(jnp.bfloat16)
        state_ref[:, pl.ds(first + width, width)] = lower.astype(jnp.bfloat16)
        return carry

    def later_flow(part, index, carry):
        f = part * half + index
        first = pl.multiple_of(f * rows, 8)
        weight = jnp.concatenate(
            [weight_ref[lane, pl.ds(first, rows), :] for lane in range(width // 128)], axis=1
        )
        stacked = jnp.concatenate(split(weight), axis=0).astype(jnp.bfloat16)
        stacked = jnp.concatenate([stacked, stacked], axis=1)
        end = state_ref[(span - 1) * scen :, pl.ds(pl.multiple_of(2 * f * width, 128), 2 * width)]
        later = lax.dot_general(stacked, end, NT, preferred_element_type=jnp.float32)
        later = later[:rows] + later[rows:]
        flow_send[part, pl.ds(index, later_rows, stride=half), :] = jnp.concatenate(
            [later[:later_rows], later[later_rows:]], axis=1
        )
        return carry

    def flow_copy(part, step):
        return pltpu.make_async_remote_copy(
            src_ref=flow_send.at[part, pl.ds((step - 1) * piece, piece)],
            dst_ref=flow_recv.at[part, step - 1],
            send_sem=flow_sems.at[0, part, step - 1],
            recv_sem=flow_sems.at[1, part, step - 1],
            device_id=(group, turn + step),
            device_id_type=MESH,
        )

    lax.fori_loop(0, per_dev, feeder_states, 0, unroll=UNROLL)
    for step in range(1, turns):

        @pl.when(turn >= step)
        def _():
            decay_copy(step).wait_send()

        @pl.when(turn + step < turns)
        def _():
            decay_copy(step).wait_recv()

    product = jnp.ones((per_dev, width), jnp.float32)
    for step in range(turns - 1):
        for t in range(span):
            product = product * later_decay[step, t]
            for k in range(2):
                row = (t % 2) * later_rows + (step * couples + t // 2) * 2 + k
                put_rows(row, maps[k] * product)

    for part in range(2):
        if turns > 1:
            lax.fori_loop(0, half, functools.partial(later_flow, part), 0, unroll=UNROLL)
        for step in range(1, turns):

            @pl.when(turn + step < turns)
            def _():
                flow_copy(part, step).start()

    local = jnp.dot(state_ref[...], column_ref[...], preferred_element_type=jnp.float32).T
    local = local[: 2 * per_dev] + local[2 * per_dev : 4 * per_dev]
    flow_ref[...] = jnp.zeros_like(flow_ref)

    effect = pair_send[group]
    for step in range(1, groups):
        pair_copy(step).wait()
        effect = effect + pair_recv[step - 1]
    effect = jnp.concatenate(
        [effect[k, part * half : (part + 1) * half] for k in range(2) for part in range(2)], axis=0
    ).T
    upper, lower = split(effect)
    effect = jnp.concatenate([upper, upper, lower], axis=1).astype(jnp.bfloat16)

    for part in range(2):
        for step in range(1, turns):

            @pl.when(turn >= step)
            def _():
                flow_copy(part, step).wait_recv()
                flow_ref[part] = flow_ref[part] + flow_recv[part, step - 1]

    for couple in range(couples):
        arrived = [
            flow_ref[part, (couple * 2 + k) * half : (couple * 2 + k + 1) * half]
            for k in range(2)
            for part in range(2)
        ]
        sources = local[:, couple * 2 * scen : (couple + 1) * 2 * scen]
        sources = sources + jnp.concatenate(arrived, axis=0)
        upper, lower = split(sources)
        sources = jnp.concatenate([upper, lower, upper], axis=0).astype(jnp.bfloat16)
        shift = jnp.dot(effect, sources, preferred_element_type=jnp.float32)
        volt_send[:, couple] = shift.reshape(groups, per_dev, 2 * scen)

    def volt_copy(step):
        target = lax.rem(group + step, groups)
        return pltpu.make_async_remote_copy(
            src_ref=volt_send.at[target],
            dst_ref=volt_recv.at[step - 1],
            send_sem=volt_sems.at[0, step - 1],
            recv_sem=volt_sems.at[1, step - 1],
            device_id=(target, turn),
            device_id_type=MESH,
        )

    for step in range(1, groups):
        volt_copy(step).start()

    mine = rule_vals[pl.ds(pl.multiple_of(group * per_dev, 8), per_dev), :]
    knot_count = knots_ref.shape[0]
    knots = [mine[:, i : i + 1] for i in range(knot_count)]
    levels = [mine[:, knot_count + i : knot_count + i + 1] for i in range(knot_count)]
    spans = [knots[i + 1] - knots[i] for i in range(knot_count - 1)]
    slopes = [(levels[i + 1] - levels[i]) / spans[i] for i in range(knot_count - 1)]
    volts = volt_send[group]
    for step in range(1, groups):
        volt_copy(step).wait_recv()
        volts = volts + volt_recv[step - 1]
    for couple in range(couples):
        value = volts[couple]
        result = levels[0] + jnp.zeros_like(value)
        for i in range(knot_count - 1):
            inside = jnp.minimum(jnp.maximum(value - knots[i], 0.0), spans[i])
            result = result + slopes[i] * inside
        out_ref[2 * couple] = result[:, :scen]
        out_ref[2 * couple + 1] = result[:, scen:]

    for step in range(1, groups):
        volt_copy(step).wait_send()
    for part in range(2):
        for step in range(1, turns):

            @pl.when(turn + step < turns)
            def _():
                flow_copy(part, step).wait_send()


def per_device(
    node_load,
    drive_map,
    decay_rate,
    counts,
    out_map,
    area_of,
    head_bus,
    rule_of,
    rule_knots,
    levels,
    sensitivity,
):
    groups, turns = lax.axis_size("feeder"), lax.axis_size("tm")
    per_dev, scen, span, nodes = node_load.shape
    width = drive_map.shape[2]
    feeders = head_bus.shape[0]
    buses = sensitivity.shape[2]
    half, couples = per_dev // 2, span // 2
    later_rows = -(-(turns - 1) * span // 8) * 8
    rows = max(2 * later_rows, 8)
    piece = couples * 2 * half
    vmem = pl.BlockSpec(memory_space=pltpu.VMEM)
    hbm = pl.BlockSpec(memory_space=pltpu.HBM)
    smem = pl.BlockSpec(memory_space=pltpu.SMEM)
    f32 = jnp.float32
    dma = pltpu.SemaphoreType.DMA
    settings = pl.pallas_call(
        functools.partial(kernel, groups, turns),
        out_shape=jax.ShapeDtypeStruct((span, per_dev, scen), f32),
        in_specs=[hbm, hbm, vmem, smem, vmem, vmem, vmem, vmem, vmem, vmem, hbm],
        out_specs=vmem,
        scratch_shapes=[
            pltpu.VMEM((per_dev, span, scen, nodes), node_load.dtype),
            pltpu.VMEM((per_dev, nodes, width), drive_map.dtype),
            pltpu.VMEM((2, buses, buses), f32),
            pltpu.VMEM((turns - 1, span, per_dev, width), f32),
            pltpu.VMEM((groups, 2, per_dev, feeders), f32),
            pltpu.VMEM((groups - 1, 2, per_dev, feeders), f32),
            pltpu.VMEM((width // 128, per_dev * rows, 128), f32),
            pltpu.VMEM((span * scen, per_dev * 2 * width), jnp.bfloat16),
            pltpu.VMEM((per_dev * 2 * width, 128), jnp.bfloat16),
            pltpu.VMEM((feeders, 2 * rule_knots.shape[1]), f32),
            pltpu.VMEM((2, piece, 2 * scen), f32),
            pltpu.VMEM((2, later_rows * half, 2 * scen), f32),
            pltpu.VMEM((2, turns - 1, piece, 2 * scen), f32),
            pltpu.VMEM((groups, couples, per_dev, 2 * scen), f32),
            pltpu.VMEM((groups - 1, couples, per_dev, 2 * scen), f32),
            dma((per_dev,)),
            dma((per_dev,)),
            dma,
            dma((2, turns - 1)),
            dma((2, groups - 1)),
            dma((2, 2, turns - 1)),
            dma((2, groups - 1)),
        ],
        compiler_params=pltpu.CompilerParams(collective_id=0, has_side_effects=True),
    )(
        jnp.transpose(node_load, (0, 2, 1, 3)),
        drive_map,
        jnp.transpose(decay_rate, (1, 0, 2)),
        counts,
        out_map,
        area_of.reshape(1, feeders),
        head_bus.reshape(1, feeders),
        rule_of.reshape(1, feeders),
        rule_knots.T,
        levels.T,
        sensitivity,
    )
    return jnp.transpose(settings, (1, 0, 2))


def solution(mesh):
    return jax.shard_map(
        per_device,
        mesh=mesh,
        in_specs=(
            P("feeder", None, "tm", None),
            P("feeder", None, None),
            P("feeder", "tm", None),
            P("feeder"),
            P("feeder", None, None),
            P(),
            P(),
            P(),
            P(),
            P(),
            P("feeder", None, None, None),
        ),
        out_specs=P("feeder", "tm", None),
        check_vma=False,
    )
```

profile of v0, /device:TPU:0, one launch (start us, length us, event | category | flops | bytes accessed | tf_op | source)
XLA Modules:
  0.0 24.6 jit_solution(16141845004619465905)
XLA Ops:
  0.0 23.2 %shard_map.109 = f32[6,16,64]{2,1,0:T(8,128)} custom-call(bf16[16,6,64,512]{3,2,1,0:T(8,128)(2,1)} %bitcast.8, bf16[16,512,256]{2,1,0:T(8,128)(2,1)} %map_hbm.1, f32[6,16,256]{2,1,0:T(8,128)} %bitcast.10, s32[16]{0:T(128)} %counts_ref.1, f32[16,2,256]{2,1,0:T(2,128)} %out_map_ref.1, s32[1,128]{1,0:T(1,128)} %bitcast.13, s32[1,128]{1,0:T(1,128)} %bitcast.14, ...), custom_call_target="tpu_custom_call" | custom-call | tf_op jit(solution)/shard_map/pallas_call | solution.py:362
  23.2 1.4 %copy.13 = f32[16,6,64]{2,0,1:T(8,128)} copy(f32[16,6,64]{2,0,1:T(8,128)} %bitcast.9) | data formatting | bytes 49152
where the time goes:
time: 24.8 us; the launch traced here: 24.6 us
  Pallas kernels  23.2 us (94%)
  local copies, waits for them, and re-layouts  1.42 us (6%)
    pallas_call x1, Pallas kernels, per_device(): pl.pallas_call(functools.partial(kernel, groups, turns), out_shape=jax.Sh...  23.2 us
    unnamed x1, local copies, waits for them, and re-layouts  1.42 us

commit v1 on v0

v1 whole, which is shorter than its diff:
```python
import functools

import jax
import jax.numpy as jnp
from jax import lax
from jax.experimental import pallas as pl
from jax.experimental.pallas import tpu as pltpu
from jax.sharding import PartitionSpec as P

HIGH = lax.Precision.HIGHEST
NT = (((1,), (1,)), ((), ()))
MESH = pl.DeviceIdType.MESH
CAP = 2
SLOT_ROWS = 8
BATCHES = 4


def split(value):
    upper = value.astype(jnp.bfloat16)
    return upper, (value - upper.astype(jnp.float32)).astype(jnp.bfloat16)


def dot(left, right):
    return jnp.dot(left, right, preferred_element_type=jnp.float32)


def dot_nt(left, right):
    return lax.dot_general(left, right, NT, preferred_element_type=jnp.float32)


def one_hot(condition):
    return jnp.where(condition, 1.0, 0.0).astype(jnp.bfloat16)


def kernel(
    groups,
    turns,
    load_hbm,
    map_hbm,
    decay_hbm,
    counts_hbm,
    out_map_hbm,
    area_hbm,
    bus_hbm,
    rule_hbm,
    knots_hbm,
    levels_hbm,
    sens_hbm,
    out_ref,
    load_ref,
    map_ref,
    sens_ref,
    decay_ref,
    counts_ref,
    out_map_ref,
    area_ref,
    bus_ref,
    rule_ref,
    knots_ref,
    levels_ref,
    later_decay,
    pair_send,
    pair_recv,
    weight_ref,
    upper_ref,
    lower_ref,
    column_ref,
    local_ref,
    rank_ref,
    rule_vals,
    flow_send,
    flow_recv,
    volt_send,
    volt_recv,
    load_sems,
    small_sems,
    decay_sems,
    pair_sems,
    flow_sems,
    volt_sems,
):
    group, turn = lax.axis_index("feeder"), lax.axis_index("tm")
    per_dev, span, scen, nodes = load_ref.shape
    width = map_ref.shape[2]
    half = per_dev // 2
    couples = span // 2
    feeders = bus_ref.shape[1]
    buses = sens_ref.shape[1]
    rows = weight_ref.shape[1] // per_dev
    later_rows = rows // 2
    piece = couples * 2 * half
    batch = per_dev // BATCHES

    barrier = pltpu.get_barrier_semaphore()
    for step in range(1, turns):
        pl.semaphore_signal(
            barrier,
            inc=1,
            device_id=(group, lax.rem(turn + step, turns)),
            device_id_type=MESH,
        )
    for step in range(1, groups):
        pl.semaphore_signal(
            barrier,
            inc=1,
            device_id=(lax.rem(group + step, groups), turn),
            device_id_type=MESH,
        )

    small = [
        pltpu.make_async_copy(source, target, small_sems.at[i])
        for i, (source, target) in enumerate(
            [
                (area_hbm, area_ref),
                (bus_hbm, bus_ref),
                (sens_hbm.at[0], sens_ref),
                (counts_hbm, counts_ref),
                (out_map_hbm, out_map_ref),
                (decay_hbm, decay_ref),
                (rule_hbm, rule_ref),
                (knots_hbm, knots_ref),
                (levels_hbm, levels_ref),
            ]
        )
    ]
    for copy in small:
        copy.start()

    def load_copies(b):
        own = pl.ds(b * batch, batch)
        return (
            pltpu.make_async_copy(map_hbm.at[own], map_ref.at[own], load_sems.at[0, b]),
            pltpu.make_async_copy(load_hbm.at[own], load_ref.at[own], load_sems.at[1, b]),
        )

    for b in range(BATCHES):
        for copy in load_copies(b):
            copy.start()

    with jax.named_scope("prep_ranks"):
        small[0].wait()
        small[1].wait()
        ids_row = lax.broadcasted_iota(jnp.int32, (feeders, feeders), 1)
        ids_col = lax.broadcasted_iota(jnp.int32, (feeders, feeders), 0)
        area_row = area_ref[...].astype(jnp.float32)
        area_col = jnp.concatenate([area_row] * 8, axis=0).T[:, :1]
        peers = (area_col == area_row) & (ids_col // per_dev == ids_row // per_dev)
        rank_row = jnp.sum(jnp.where(peers & (ids_col < ids_row), 1.0, 0.0), axis=0, keepdims=True)
        rank_ref[...] = jnp.concatenate([area_row] * 4 + [rank_row] * 4, axis=0).T

        place = lax.broadcasted_iota(jnp.int32, (groups * SLOT_ROWS, feeders), 0)
        owner = lax.broadcasted_iota(jnp.int32, (groups * SLOT_ROWS, feeders), 1) // per_dev
        slot = lax.rem(place, SLOT_ROWS)
        wanted = (place // SLOT_ROWS == owner) & (area_ref[...] == group) & (slot < 2 * CAP)
        chosen = one_hot(wanted & (rank_row == lax.rem(slot, CAP).astype(jnp.float32)))
        bus_ids = lax.broadcasted_iota(jnp.int32, (buses, feeders), 0)
        owned = (bus_ids == bus_ref[...]) & (area_ref[...] == group)
        hot = one_hot(owned)
        sources = dot_nt(chosen, hot).astype(jnp.bfloat16)

    with jax.named_scope("prep_pairs"):
        small[2].wait()
        picked = [sum(dot_nt(sources, term) for term in split(sens_ref[k])) for k in range(2)]
        kind = lax.broadcasted_iota(jnp.int32, (groups * SLOT_ROWS, buses), 0)
        kind = lax.rem(kind, SLOT_ROWS) // CAP
        picked = jnp.where(kind == 0, picked[0], picked[1])
        pairs = sum(dot(term, hot) for term in split(picked))
        pair_send[...] = pairs.reshape(groups, SLOT_ROWS, feeders)

    def decay_copy(part, step):
        own = pl.ds(part * half, half)
        return pltpu.make_async_remote_copy(
            src_ref=decay_hbm.at[:, own],
            dst_ref=later_decay.at[step - 1, :, own],
            send_sem=decay_sems.at[0, part, step - 1],
            recv_sem=decay_sems.at[1, part, step - 1],
            device_id=(group, turn - step),
            device_id_type=MESH,
        )

    def pair_copy(step):
        target = lax.rem(group + step, groups)
        return pltpu.make_async_remote_copy(
            src_ref=pair_send.at[target],
            dst_ref=pair_recv.at[step],
            send_sem=pair_sems.at[0, step - 1],
            recv_sem=pair_sems.at[1, step - 1],
            device_id=(target, turn),
            device_id_type=MESH,
        )

    with jax.named_scope("barrier"):
        pl.semaphore_wait(barrier, turns + groups - 2)
    for part in range(2):
        for step in range(1, turns):

            @pl.when(turn >= step)
            def _():
                decay_copy(part, step).start()

    for step in range(1, groups):
        pair_copy(step).start()

    with jax.named_scope("prep_columns"):
        small[3].wait()
        small[4].wait()
        small[5].wait()
        same = lax.broadcasted_iota(jnp.int32, (per_dev, per_dev), 0) == lax.broadcasted_iota(
            jnp.int32, (per_dev, per_dev), 1
        )
        limit = jnp.sum(
            jnp.where(same, counts_ref[...].astype(jnp.float32), 0.0), axis=1, keepdims=True
        )
        state_ids = lax.broadcasted_iota(jnp.int32, (per_dev, width), 1).astype(jnp.float32)
        maps = [jnp.where(state_ids < limit, out_map_ref[:, k, :], 0.0) for k in range(2)]
        parts = [split(m) for m in maps]
        columns = [p[0] for p in parts] + [p[1] for p in parts]
        blank = jnp.zeros((128 - 4 * per_dev, width), jnp.float32)
        columns = [c.astype(jnp.float32) for c in columns] + [blank]
        columns = jnp.concatenate(columns, axis=0).T.astype(jnp.bfloat16)
        lane_ids = lax.rem(lax.broadcasted_iota(jnp.int32, (1, 128), 1), per_dev)
        for f in range(per_dev):
            column_ref[f * width : (f + 1) * width] = columns * one_hot(lane_ids == f)

    def states(b):
        for copy in load_copies(b):
            copy.wait()
        for f in range(b * batch, (b + 1) * batch):
            drive = dot(load_ref[f].reshape(span * scen, nodes), map_ref[f])
            state = drive[:scen]
            own = slice(f * width, (f + 1) * width)
            for t in range(span):
                now = slice(t * scen, (t + 1) * scen)
                if t:
                    state = decay_ref[t, f : f + 1, :] * state + drive[now]
                upper_ref[now, own], lower_ref[now, own] = split(state)

    def local_flow(b):
        own = slice(b * batch * width, (b + 1) * batch * width)
        value = dot(upper_ref[:, own], column_ref[own]) + dot(lower_ref[:, own], column_ref[own])
        local_ref[...] = value if b == 0 else local_ref[...] + value

    with jax.named_scope("states0"):
        states(0)

    for b in range(1, BATCHES):
        with jax.named_scope("states%d" % b):
            states(b)
            local_flow(b - 1)

    def put_rows(row, value):
        for lane in range(width // 128):
            weight_ref[lane, pl.ds(row, half, stride=rows), :] = value[
                :, lane * 128 : (lane + 1) * 128
            ]

    def products(part):
        own = slice(part * half, (part + 1) * half)
        product = jnp.ones((half, width), jnp.float32)
        for step in range(turns - 1):
            for t in range(span):
                product = product * later_decay[step, t, own]
                for k in range(2):
                    row = (t % 2) * later_rows + (step * couples + t // 2) * 2 + k
                    put_rows(part * half * rows + row, maps[k][own] * product)

    end = slice((span - 1) * scen, span * scen)

    def later_flow(part):
        for index in range(half):
            f = part * half + index
            weight = jnp.concatenate(
                [weight_ref[lane, f * rows : (f + 1) * rows, :] for lane in range(width // 128)],
                axis=1,
            )
            stacked = jnp.concatenate(split(weight), axis=0)
            own = slice(f * width, (f + 1) * width)
            later = dot_nt(stacked, upper_ref[end, own]) + dot_nt(stacked, lower_ref[end, own])
            later = later[:rows] + later[rows:]
            flow_send[part, pl.ds(index, later_rows, stride=half), :] = jnp.concatenate(
                [later[:later_rows], later[later_rows:]], axis=1
            )

    def flow_copy(part, step):
        return pltpu.make_async_remote_copy(
            src_ref=flow_send.at[part, pl.ds((step - 1) * piece, piece)],
            dst_ref=flow_recv.at[part, step - 1],
            send_sem=flow_sems.at[0, part, step - 1],
            recv_sem=flow_sems.at[1, part, step - 1],
            device_id=(group, turn + step),
            device_id_type=MESH,
        )

    def send_flow(part):
        for step in range(1, turns):

            @pl.when(turn + step < turns)
            def _():
                flow_copy(part, step).start()

    for part in range(2):
        with jax.named_scope("decaywait%d" % part):
            for step in range(1, turns):

                @pl.when(turn >= step)
                def _():
                    decay_copy(part, step).wait_send()

                @pl.when(turn + step < turns)
                def _():
                    decay_copy(part, step).wait_recv()

        if turns > 1:
            with jax.named_scope("later%d" % part):
                products(part)
                later_flow(part)
        send_flow(part)

    with jax.named_scope("local_last"):
        local_flow(BATCHES - 1)
        local = local_ref[...].T
        local = local[: 2 * per_dev] + local[2 * per_dev : 4 * per_dev]

    with jax.named_scope("rules"):
        for copy in small[6:]:
            copy.wait()
        rules = knots_ref.shape[1]
        rule_ids = lax.broadcasted_iota(jnp.int32, (rules, feeders), 0)
        rule_hot = jnp.where(rule_ids == rule_ref[...], 1.0, 0.0)
        table = jnp.concatenate(
            [knots_ref[...].astype(jnp.float32), levels_ref[...].astype(jnp.float32)], axis=0
        )
        chosen = jnp.dot(table, rule_hot, precision=HIGH, preferred_element_type=jnp.float32)
        rule_vals[...] = (chosen / 1000.0).T

    with jax.named_scope("effect"):
        pair_recv[0] = pair_send[group]
        for step in range(1, groups):
            pair_copy(step).wait()
        places = groups * SLOT_ROWS
        mine = rank_ref[pl.ds(pl.multiple_of(group * per_dev, 8), per_dev), :]
        mine = jnp.concatenate([mine, mine], axis=0)
        place = lax.broadcasted_iota(jnp.int32, (2 * per_dev, places), 1)
        kind = lax.broadcasted_iota(jnp.int32, (2 * per_dev, places), 0) // per_dev
        source = lax.rem(group + groups - place // SLOT_ROWS, groups).astype(jnp.float32)
        slot = lax.rem(place, SLOT_ROWS)
        taken = (mine[:, :1] == source) & (slot // CAP == kind)
        taken = one_hot(taken & (mine[:, 4:5] == lax.rem(slot, CAP).astype(jnp.float32)))
        upper, lower = [
            dot(taken, term).T.astype(jnp.bfloat16)
            for term in split(pair_recv[...].reshape(places, feeders))
        ]
        effect = jnp.concatenate([upper, upper, lower], axis=1)

    with jax.named_scope("flowwait"):
        for part in range(2):
            for step in range(1, turns):

                @pl.when(turn >= step)
                def _():
                    flow_copy(part, step).wait_recv()

                @pl.when(turn < step)
                def _():
                    flow_recv[part, step - 1] = jnp.zeros((piece, 2 * scen), jnp.float32)

    def volt_copy(step):
        target = lax.rem(group + step, groups)
        return pltpu.make_async_remote_copy(
            src_ref=volt_send.at[target],
            dst_ref=volt_recv.at[step - 1],
            send_sem=volt_sems.at[0, step - 1],
            recv_sem=volt_sems.at[1, step - 1],
            device_id=(target, turn),
            device_id_type=MESH,
        )

    with jax.named_scope("shift"):
        arrived = [
            sum(flow_recv[part, step] for step in range(turns - 1))
            if turns > 1
            else jnp.zeros((piece, 2 * scen), jnp.float32)
            for part in range(2)
        ]
        for couple in range(couples):
            extra = [
                arrived[part][(couple * 2 + k) * half : (couple * 2 + k + 1) * half]
                for k in range(2)
                for part in range(2)
            ]
            sources = local[:, couple * 2 * scen : (couple + 1) * 2 * scen]
            upper, lower = split(sources + jnp.concatenate(extra, axis=0))
            sources = jnp.concatenate([upper, lower, upper], axis=0)
            volt_send[:, couple] = dot(effect, sources).reshape(groups, per_dev, 2 * scen)

    for step in range(1, groups):
        volt_copy(step).start()

    mine = rule_vals[pl.ds(pl.multiple_of(group * per_dev, 8), per_dev), :]
    knot_count = knots_ref.shape[0]
    knots = [mine[:, i : i + 1] for i in range(knot_count)]
    levels = [mine[:, knot_count + i : knot_count + i + 1] for i in range(knot_count)]
    spans = [knots[i + 1] - knots[i] for i in range(knot_count - 1)]
    slopes = [(levels[i + 1] - levels[i]) / spans[i] for i in range(knot_count - 1)]
    with jax.named_scope("voltwait"):
        volts = volt_send[group]
        for step in range(1, groups):
            volt_copy(step).wait_recv()
            volts = volts + volt_recv[step - 1]
    with jax.named_scope("rule"):
        for couple in range(couples):
            value = volts[couple]
            result = levels[0] + jnp.zeros_like(value)
            for i in range(knot_count - 1):
                inside = jnp.minimum(jnp.maximum(value - knots[i], 0.0), spans[i])
                result = result + slopes[i] * inside
            out_ref[2 * couple] = result[:, :scen]
            out_ref[2 * couple + 1] = result[:, scen:]

    for step in range(1, groups):
        volt_copy(step).wait_send()
    for part in range(2):
        for step in range(1, turns):

            @pl.when(turn + step < turns)
            def _():
                flow_copy(part, step).wait_send()


def per_device(
    node_load,
    drive_map,
    decay_rate,
    counts,
    out_map,
    area_of,
    head_bus,
    rule_of,
    rule_knots,
    levels,
    sensitivity,
):
    groups, turns = lax.axis_size("feeder"), lax.axis_size("tm")
    per_dev, scen, span, nodes = node_load.shape
    width = drive_map.shape[2]
    feeders = head_bus.shape[0]
    buses = sensitivity.shape[2]
    half, couples = per_dev // 2, span // 2
    later_rows = -(-(turns - 1) * span // 8) * 8
    rows = max(2 * later_rows, 8)
    piece = couples * 2 * half
    vmem = pl.BlockSpec(memory_space=pltpu.VMEM)
    hbm = pl.BlockSpec(memory_space=pltpu.HBM)
    f32, i32 = jnp.float32, jnp.int32
    dma = pltpu.SemaphoreType.DMA
    operands = (
        jnp.transpose(node_load, (0, 2, 1, 3)),
        drive_map,
        jnp.transpose(decay_rate, (1, 0, 2)),
        counts.reshape(1, per_dev),
        out_map,
        area_of.reshape(1, feeders),
        head_bus.reshape(1, feeders),
        rule_of.reshape(1, feeders),
        rule_knots.T,
        levels.T,
        sensitivity,
    )
    settings = pl.pallas_call(
        functools.partial(kernel, groups, turns),
        out_shape=jax.ShapeDtypeStruct((span, per_dev, scen), f32),
        in_specs=[hbm] * len(operands),
        out_specs=vmem,
        scratch_shapes=[
            pltpu.VMEM((per_dev, span, scen, nodes), node_load.dtype),
            pltpu.VMEM((per_dev, nodes, width), drive_map.dtype),
            pltpu.VMEM((2, buses, buses), f32),
            pltpu.VMEM((span, per_dev, width), f32),
            pltpu.VMEM((1, per_dev), i32),
            pltpu.VMEM(out_map.shape, f32),
            pltpu.VMEM((1, feeders), i32),
            pltpu.VMEM((1, feeders), i32),
            pltpu.VMEM((1, feeders), i32),
            pltpu.VMEM(rule_knots.shape[::-1], i32),
            pltpu.VMEM(levels.shape[::-1], i32),
            pltpu.VMEM((turns - 1, span, per_dev, width), f32),
            pltpu.VMEM((groups, SLOT_ROWS, feeders), f32),
            pltpu.VMEM((groups, SLOT_ROWS, feeders), f32),
            pltpu.VMEM((width // 128, per_dev * rows, 128), f32),
            pltpu.VMEM((span * scen, per_dev * width), jnp.bfloat16),
            pltpu.VMEM((span * scen, per_dev * width), jnp.bfloat16),
            pltpu.VMEM((per_dev * width, 128), jnp.bfloat16),
            pltpu.VMEM((span * scen, 128), f32),
            pltpu.VMEM((feeders, 8), f32),
            pltpu.VMEM((feeders, 2 * rule_knots.shape[1]), f32),
            pltpu.VMEM((2, later_rows * half, 2 * scen), f32),
            pltpu.VMEM((2, turns - 1, piece, 2 * scen), f32),
            pltpu.VMEM((groups, couples, per_dev, 2 * scen), f32),
            pltpu.VMEM((groups - 1, couples, per_dev, 2 * scen), f32),
            dma((2, BATCHES)),
            dma((9,)),
            dma((2, 2, turns - 1)),
            dma((2, groups - 1)),
            dma((2, 2, turns - 1)),
            dma((2, groups - 1)),
        ],
        compiler_params=pltpu.CompilerParams(
            collective_id=0, has_side_effects=True, vmem_limit_bytes=VMEM_LIMIT
        ),
    )(*[pltpu.with_memory_space_constraint(x, pltpu.HBM) for x in operands])
    return jnp.transpose(settings, (1, 0, 2))


VMEM_LIMIT = 48 * 2**20


def solution(mesh):
    return jax.shard_map(
        per_device,
        mesh=mesh,
        in_specs=(
            P("feeder", None, "tm", None),
            P("feeder", None, None),
            P("feeder", "tm", None),
            P("feeder"),
            P("feeder", None, None),
            P(),
            P(),
            P(),
            P(),
            P(),
            P("feeder", None, None, None),
        ),
        out_specs=P("feeder", "tm", None),
        check_vma=False,
    )
```

time: 24.8 us -> 20.5 us (0.83)
  Pallas kernels: 23.2 us -> 19.7 us
  local copies, waits for them, and re-layouts: 1.42 us -> 0.62 us
    pallas_call x1, Pallas kernels: 23.2 us -> 19.7 us  [per_device(): pl.pallas_call(functools.partial(kernel, groups, turns), out_shape=jax.Sh...]
    unnamed x1, local copies, waits for them, and re-layouts: 1.42 us -> 0.62 us
where the time goes in v1:
time: 20.5 us; the launch traced here: 20.4 us
  Pallas kernels  19.7 us (96%)
  local copies, waits for them, and re-layouts  0.62 us (3%)
    pallas_call x1, Pallas kernels, per_device(): pl.pallas_call(functools.partial(kernel, groups, turns), out_shape=jax.Sh...  19.7 us
    unnamed x1, local copies, waits for them, and re-layouts  0.62 us

profile of v1, /device:TPU:0, one launch (start us, length us, event | category | flops | bytes accessed | tf_op | source)
XLA Modules:
  0.0 20.4 jit_solution(16325918526236936944)
XLA Ops:
  0.0 19.7 %shard_map.109 = f32[6,16,64]{2,1,0:T(8,128)S(1)} custom-call(bf16[16,6,64,512]{3,2,1,0:T(8,128)(2,1)} %bitcast.10, bf16[16,512,256]{2,1,0:T(8,128)(2,1)} %map_hbm.1, f32[6,16,256]{2,1,0:T(8,128)} %bitcast.11, s32[1,16]{1,0:T(1,128)} %bitcast.14, f32[16,2,256]{2,1,0:T(2,128)} %out_map_hbm.1, s32[1,128]{1,0:T(1,128)} %bitcast.15, s32[1,128]{1,0:T(1,128)} %bitcast.16, ...), custom_call_target="tpu_custom_call" | custom-call | tf_op jit(solution)/shard_map/pallas_call | solution.py:469
  19.7 0.6 %copy.13 = f32[16,6,64]{2,0,1:T(8,128)} copy(f32[16,6,64]{2,0,1:T(8,128)S(1)} %bitcast.9) | data formatting | bytes 49152

commit v2 on v1

--- a/solution.py
+++ b/solution.py
@@ -13,6 +13,7 @@
 CAP = 2
 SLOT_ROWS = 8
 BATCHES = 4
+NEAR = 2
 
 
 def split(value):
@@ -62,8 +63,7 @@
     pair_send,
     pair_recv,
     weight_ref,
-    upper_ref,
-    lower_ref,
+    state_ref,
     column_ref,
     local_ref,
     rank_ref,
@@ -74,6 +74,7 @@
     volt_recv,
     load_sems,
     small_sems,
+    reach_sems,
     decay_sems,
     pair_sems,
     flow_sems,
@@ -99,24 +100,37 @@
             device_id=(group, lax.rem(turn + step, turns)),
             device_id_type=MESH,
         )
-    for step in range(1, groups):
-        pl.semaphore_signal(
-            barrier,
-            inc=1,
-            device_id=(lax.rem(group + step, groups), turn),
-            device_id_type=MESH,
-        )
+
+    def tell(semaphore, distance):
+        @pl.when(group + distance < groups)
+        def _():
+            pl.semaphore_signal(
+                semaphore, inc=1, device_id=(group + distance, turn), device_id_type=MESH
+            )
+
+        @pl.when(group >= distance)
+        def _():
+            pl.semaphore_signal(
+                semaphore, inc=1, device_id=(group - distance, turn), device_id_type=MESH
+            )
+
+    def tellers(distance):
+        above = lax.div(2 * groups - 1 - group - distance, groups)
+        return above + lax.div(groups + group - distance, groups)
+
+    for distance in range(1, min(NEAR, groups - 1) + 1):
+        tell(barrier, distance)
 
     small = [
         pltpu.make_async_copy(source, target, small_sems.at[i])
         for i, (source, target) in enumerate(
             [
+                (decay_hbm, decay_ref),
                 (area_hbm, area_ref),
                 (bus_hbm, bus_ref),
                 (sens_hbm.at[0], sens_ref),
                 (counts_hbm, counts_ref),
                 (out_map_hbm, out_map_ref),
-                (decay_hbm, decay_ref),
                 (rule_hbm, rule_ref),
                 (knots_hbm, knots_ref),
                 (levels_hbm, levels_ref),
@@ -133,13 +147,26 @@
             pltpu.make_async_copy(load_hbm.at[own], load_ref.at[own], load_sems.at[1, b]),
         )
 
-    for b in range(BATCHES):
-        for copy in load_copies(b):
-            copy.start()
+    for copy in load_copies(0):
+        copy.start()
+
+    def decay_copy(part, step):
+        own = pl.ds(part * half, half)
+        return pltpu.make_async_remote_copy(
+            src_ref=decay_ref.at[:, own],
+            dst_ref=later_decay.at[step - 1, :, own],
+            send_sem=decay_sems.at[0, part, step - 1],
+            recv_sem=decay_sems.at[1, part, step - 1],
+            device_id=(group, turn - step),
+            device_id_type=MESH,
+        )
 
     with jax.named_scope("prep_ranks"):
-        small[0].wait()
         small[1].wait()
+        small[2].wait()
+        for b in range(1, BATCHES):
+            for copy in load_copies(b):
+                copy.start()
         ids_row = lax.broadcasted_iota(jnp.int32, (feeders, feeders), 1)
         ids_col = lax.broadcasted_iota(jnp.int32, (feeders, feeders), 0)
         area_row = area_ref[...].astype(jnp.float32)
@@ -158,25 +185,28 @@
         hot = one_hot(owned)
         sources = dot_nt(chosen, hot).astype(jnp.bfloat16)
 
+    with jax.named_scope("barrier"):
+        near = [tellers(distance) for distance in range(1, min(NEAR, groups - 1) + 1)]
+        pl.semaphore_wait(barrier, turns - 1 + sum(near))
+    reach = [NEAR << i for i in range(groups) if NEAR << i < groups]
+    if reach:
+        tell(reach_sems.at[0], reach[0])
+    small[0].wait()
+    for part in range(2):
+        for step in range(turns - 1, 0, -1):
+
+            @pl.when(turn >= step)
+            def _():
+                decay_copy(part, step).start()
+
     with jax.named_scope("prep_pairs"):
-        small[2].wait()
+        small[3].wait()
         picked = [sum(dot_nt(sources, term) for term in split(sens_ref[k])) for k in range(2)]
         kind = lax.broadcasted_iota(jnp.int32, (groups * SLOT_ROWS, buses), 0)
         kind = lax.rem(kind, SLOT_ROWS) // CAP
         picked = jnp.where(kind == 0, picked[0], picked[1])
         pairs = sum(dot(term, hot) for term in split(picked))
         pair_send[...] = pairs.reshape(groups, SLOT_ROWS, feeders)
-
-    def decay_copy(part, step):
-        own = pl.ds(part * half, half)
-        return pltpu.make_async_remote_copy(
-            src_ref=decay_hbm.at[:, own],
-            dst_ref=later_decay.at[step - 1, :, own],
-            send_sem=decay_sems.at[0, part, step - 1],
-            recv_sem=decay_sems.at[1, part, step - 1],
-            device_id=(group, turn - step),
-            device_id_type=MESH,
-        )
 
     def pair_copy(step):
         target = lax.rem(group + step, groups)
@@ -189,20 +219,7 @@
             device_id_type=MESH,
         )
 
-    with jax.named_scope("barrier"):
-        pl.semaphore_wait(barrier, turns + groups - 2)
-    for part in range(2):
-        for step in range(1, turns):
-
-            @pl.when(turn >= step)
-            def _():
-                decay_copy(part, step).start()
-
-    for step in range(1, groups):
-        pair_copy(step).start()
-
-    with jax.named_scope("prep_columns"):
-        small[3].wait()
+    with jax.named_scope("prep_maps"):
         small[4].wait()
         small[5].wait()
         same = lax.broadcasted_iota(jnp.int32, (per_dev, per_dev), 0) == lax.broadcasted_iota(
@@ -213,6 +230,8 @@
         )
         state_ids = lax.broadcasted_iota(jnp.int32, (per_dev, width), 1).astype(jnp.float32)
         maps = [jnp.where(state_ids < limit, out_map_ref[:, k, :], 0.0) for k in range(2)]
+
+    with jax.named_scope("columns"):
         parts = [split(m) for m in maps]
         columns = [p[0] for p in parts] + [p[1] for p in parts]
         blank = jnp.zeros((128 - 4 * per_dev, width), jnp.float32)
@@ -226,27 +245,48 @@
         for copy in load_copies(b):
             copy.wait()
         for f in range(b * batch, (b + 1) * batch):
-            drive = dot(load_ref[f].reshape(span * scen, nodes), map_ref[f])
-            state = drive[:scen]
             own = slice(f * width, (f + 1) * width)
-            for t in range(span):
-                now = slice(t * scen, (t + 1) * scen)
-                if t:
-                    state = decay_ref[t, f : f + 1, :] * state + drive[now]
-                upper_ref[now, own], lower_ref[now, own] = split(state)
+            state = None
+            for part in range(2):
+                first = part * couples
+                load = load_ref[f, couples:] if part else load_ref[f, :couples]
+                drive = dot(load.reshape(load.shape[0] * scen, nodes), map_ref[f])
+                for t in range(load.shape[0]):
+                    push = drive[t * scen : (t + 1) * scen]
+                    row = (first + t) * scen
+                    if state is None:
+                        state = push
+                    else:
+                        state = decay_ref[first + t, f : f + 1, :] * state + push
+                    upper, lower = split(state)
+                    state_ref[row : row + scen, own] = upper
+                    state_ref[span * scen + row : span * scen + row + scen, own] = lower
 
     def local_flow(b):
         own = slice(b * batch * width, (b + 1) * batch * width)
-        value = dot(upper_ref[:, own], column_ref[own]) + dot(lower_ref[:, own], column_ref[own])
-        local_ref[...] = value if b == 0 else local_ref[...] + value
-
-    with jax.named_scope("states0"):
-        states(0)
-
-    for b in range(1, BATCHES):
+        upper = dot(state_ref[: span * scen, own], column_ref[own])
+        value = upper + dot(state_ref[span * scen :, own], column_ref[own])
+        local_ref[...] = local_ref[...] + value if b else value
+
+    def pass_on(i):
+        with jax.named_scope("reach%d" % i):
+            pl.semaphore_wait(reach_sems.at[i], tellers(reach[i]))
+        if i + 1 < len(reach):
+            tell(reach_sems.at[i + 1], reach[i + 1])
+
+    last = BATCHES - 2
+    rounds = [max(0, last - (len(reach) - 1 - i)) if i else 0 for i in range(len(reach))]
+    for b in range(BATCHES):
         with jax.named_scope("states%d" % b):
             states(b)
-            local_flow(b - 1)
+            if b:
+                local_flow(b - 1)
+        for i, place in enumerate(rounds):
+            if place == b:
+                pass_on(i)
+        if b == last:
+            for step in range(1, groups):
+                pair_copy(step).start()
 
     def put_rows(row, value):
         for lane in range(width // 128):
@@ -264,7 +304,7 @@
                     row = (t % 2) * later_rows + (step * couples + t // 2) * 2 + k
                     put_rows(part * half * rows + row, maps[k][own] * product)
 
-    end = slice((span - 1) * scen, span * scen)
+    end = [slice((n * span - 1) * scen, n * span * scen) for n in (1, 2)]
 
     def later_flow(part):
         for index in range(half):
@@ -275,7 +315,7 @@
             )
             stacked = jnp.concatenate(split(weight), axis=0)
             own = slice(f * width, (f + 1) * width)
-            later = dot_nt(stacked, upper_ref[end, own]) + dot_nt(stacked, lower_ref[end, own])
+            later = dot_nt(stacked, state_ref[end[0], own]) + dot_nt(stacked, state_ref[end[1], own])
             later = later[:rows] + later[rows:]
             flow_send[part, pl.ds(index, later_rows, stride=half), :] = jnp.concatenate(
                 [later[:later_rows], later[later_rows:]], axis=1
@@ -320,18 +360,6 @@
         local_flow(BATCHES - 1)
         local = local_ref[...].T
         local = local[: 2 * per_dev] + local[2 * per_dev : 4 * per_dev]
-
-    with jax.named_scope("rules"):
-        for copy in small[6:]:
-            copy.wait()
-        rules = knots_ref.shape[1]
-        rule_ids = lax.broadcasted_iota(jnp.int32, (rules, feeders), 0)
-        rule_hot = jnp.where(rule_ids == rule_ref[...], 1.0, 0.0)
-        table = jnp.concatenate(
-            [knots_ref[...].astype(jnp.float32), levels_ref[...].astype(jnp.float32)], axis=0
-        )
-        chosen = jnp.dot(table, rule_hot, precision=HIGH, preferred_element_type=jnp.float32)
-        rule_vals[...] = (chosen / 1000.0).T
 
     with jax.named_scope("effect"):
         pair_recv[0] = pair_send[group]
@@ -364,14 +392,26 @@
                 def _():
                     flow_recv[part, step - 1] = jnp.zeros((piece, 2 * scen), jnp.float32)
 
-    def volt_copy(step):
-        target = lax.rem(group + step, groups)
+    def other(k):
+        return k + lax.div(groups + k - group, groups)
+
+    def volt_copy(k):
         return pltpu.make_async_remote_copy(
-            src_ref=volt_send.at[target],
-            dst_ref=volt_recv.at[step - 1],
-            send_sem=volt_sems.at[0, step - 1],
-            recv_sem=volt_sems.at[1, step - 1],
-            device_id=(target, turn),
+            src_ref=volt_send.at[other(k)],
+            dst_ref=volt_recv.at[group],
+            send_sem=volt_sems.at[0, k],
+            recv_sem=volt_sems.at[1, group],
+            device_id=(other(k), turn),
+            device_id_type=MESH,
+        )
+
+    def volt_arrival(k):
+        return pltpu.make_async_remote_copy(
+            src_ref=volt_send.at[other(k)],
+            dst_ref=volt_recv.at[other(k)],
+            send_sem=volt_sems.at[0, k],
+            recv_sem=volt_sems.at[1, other(k)],
+            device_id=(other(k), turn),
             device_id_type=MESH,
         )
 
@@ -393,8 +433,20 @@
             sources = jnp.concatenate([upper, lower, upper], axis=0)
             volt_send[:, couple] = dot(effect, sources).reshape(groups, per_dev, 2 * scen)
 
-    for step in range(1, groups):
-        volt_copy(step).start()
+    for k in range(groups - 1):
+        volt_copy(k).start()
+
+    with jax.named_scope("rules"):
+        for copy in small[6:]:
+            copy.wait()
+        rules = knots_ref.shape[1]
+        rule_ids = lax.broadcasted_iota(jnp.int32, (rules, feeders), 0)
+        rule_hot = jnp.where(rule_ids == rule_ref[...], 1.0, 0.0)
+        table = jnp.concatenate(
+            [knots_ref[...].astype(jnp.float32), levels_ref[...].astype(jnp.float32)], axis=0
+        )
+        chosen = jnp.dot(table, rule_hot, precision=HIGH, preferred_element_type=jnp.float32)
+        rule_vals[...] = (chosen / 1000.0).T
 
     mine = rule_vals[pl.ds(pl.multiple_of(group * per_dev, 8), per_dev), :]
     knot_count = knots_ref.shape[0]
@@ -404,9 +456,9 @@
     slopes = [(levels[i + 1] - levels[i]) / spans[i] for i in range(knot_count - 1)]
     with jax.named_scope("voltwait"):
         volts = volt_send[group]
-        for step in range(1, groups):
-            volt_copy(step).wait_recv()
-            volts = volts + volt_recv[step - 1]
+        for k in range(groups - 1):
+            volt_arrival(k).wait_recv()
+            volts = volts + volt_recv[other(k)]
     with jax.named_scope("rule"):
         for couple in range(couples):
             value = volts[couple]
@@ -417,8 +469,8 @@
             out_ref[2 * couple] = result[:, :scen]
             out_ref[2 * couple + 1] = result[:, scen:]
 
-    for step in range(1, groups):
-        volt_copy(step).wait_send()
+    for k in range(groups - 1):
+        volt_copy(k).wait_send()
     for part in range(2):
         for step in range(1, turns):
 
@@ -487,8 +539,7 @@
             pltpu.VMEM((groups, SLOT_ROWS, feeders), f32),
             pltpu.VMEM((groups, SLOT_ROWS, feeders), f32),
             pltpu.VMEM((width // 128, per_dev * rows, 128), f32),
-            pltpu.VMEM((span * scen, per_dev * width), jnp.bfloat16),
-            pltpu.VMEM((span * scen, per_dev * width), jnp.bfloat16),
+            pltpu.VMEM((2 * span * scen, per_dev * width), jnp.bfloat16),
             pltpu.VMEM((per_dev * width, 128), jnp.bfloat16),
             pltpu.VMEM((span * scen, 128), f32),
             pltpu.VMEM((feeders, 8), f32),
@@ -496,13 +547,14 @@
             pltpu.VMEM((2, later_rows * half, 2 * scen), f32),
             pltpu.VMEM((2, turns - 1, piece, 2 * scen), f32),
             pltpu.VMEM((groups, couples, per_dev, 2 * scen), f32),
-            pltpu.VMEM((groups - 1, couples, per_dev, 2 * scen), f32),
+            pltpu.VMEM((groups, couples, per_dev, 2 * scen), f32),
             dma((2, BATCHES)),
             dma((9,)),
+            pltpu.SemaphoreType.REGULAR((8,)),
             dma((2, 2, turns - 1)),
             dma((2, groups - 1)),
             dma((2, 2, turns - 1)),
-            dma((2, groups - 1)),
+            dma((2, groups)),
         ],
         compiler_params=pltpu.CompilerParams(
             collective_id=0, has_side_effects=True, vmem_limit_bytes=VMEM_LIMIT

time: 20.5 us -> 20.4 us (level)
  the two profiles are of different devices: /device:TPU:0 before, /device:TPU:5 now
where the time goes in v2:
time: 20.4 us; the launch traced here: 20.2 us
  Pallas kernels  19.6 us (96%)
  local copies, waits for them, and re-layouts  0.62 us (3%)
    pallas_call x1, Pallas kernels, per_device(): pl.pallas_call(functools.partial(kernel, groups, turns), out_shape=jax.Sh...  19.6 us
    unnamed x1, local copies, waits for them, and re-layouts  0.62 us

profile of v2, /device:TPU:5, one launch (start us, length us, event | category | flops | bytes accessed | tf_op | source)
XLA Modules:
  0.0 20.2 jit_solution(918903860588764584)
XLA Ops:
  0.0 19.6 %shard_map.109 = f32[6,16,64]{2,1,0:T(8,128)S(1)} custom-call(bf16[16,6,64,512]{3,2,1,0:T(8,128)(2,1)} %bitcast.10, bf16[16,512,256]{2,1,0:T(8,128)(2,1)} %map_hbm.1, f32[6,16,256]{2,1,0:T(8,128)} %bitcast.11, s32[1,16]{1,0:T(1,128)} %bitcast.14, f32[16,2,256]{2,1,0:T(2,128)} %out_map_hbm.1, s32[1,128]{1,0:T(1,128)} %bitcast.15, s32[1,128]{1,0:T(1,128)} %bitcast.16, ...), custom_call_target="tpu_custom_call" | custom-call | tf_op jit(solution)/shard_map/pallas_call | solution.py:521
  19.6 0.6 %copy.13 = f32[16,6,64]{2,0,1:T(8,128)} copy(f32[16,6,64]{2,0,1:T(8,128)S(1)} %bitcast.9) | data formatting | bytes 49152
